TPU v7x, 32 devices: a whole 2x2x4 slice. The times are simulated.
32 devices in a mesh: lat: 4 (over y, x), lon: 8 (over z, core).
Axes of the slice: x: 2, y: 2, z: 4, core: 2. Of those that a mesh axis runs over, the one named last changes fastest.
Arguments:
- departures: bfloat16 [65536, 256], P(('lat', 'lon')), may hold values from -6 to 6
- footprint: int32 [65536, 4], P(('lat', 'lon')), may hold values from 0 to 131071, as said below
- channel_map: bfloat16 [256, 128], replicated, may hold values from -0.375 to 0.375
- adjoint_in: float32 [128, 128, 1024], P(None, 'lat', 'lon'), may hold values from -6 to 6
- wind_lon: float32 [128, 128, 1024], P(None, 'lat', 'lon'), may hold values from -0.4 to 0.4
- wind_lat: float32 [128, 128, 1024], P(None, 'lat', 'lon'), may hold values from -0.4 to 0.4
Outputs:
- adjoint_out: float32 [128, 128, 1024], P(None, 'lat', 'lon')
Inputs may be any that keep to these rules, and one draw needn't show every extreme that they name: `footprint`: the 4 columns of an observation form a 2 by 2 block of neighbouring columns that lie in one device's block of 32 x 128 columns (wrapping inside that block). The observations of one holder device fall into at most 128 per owner device, and in every holder's rows some owner device receives exactly 128.
All inputs are finite; a program needn't handle non-finite values.
Results may differ from a plain program's by a relative error of at most 0.0015.
Values may be sent and summed in bfloat16 or wider, within the bound.
A program may use at most 64 MiB of HBM per device.

v0:
```python
import functools

import jax
import jax.numpy as jnp
from jax import lax
from jax.experimental import pallas as pl
from jax.experimental.pallas import tpu as pltpu
from jax.sharding import PartitionSpec as P

STEPS = 2
RATE = 0.2
LANES = 128
META = 16
MESH = pl.DeviceIdType.MESH


def log2(size):
    assert size & (size - 1) == 0
    return size.bit_length() - 1


def nt_dot(a, b):
    return lax.dot_general(a, b, (((1,), (1,)), ((), ())), preferred_element_type=jnp.float32)


def kernel(
    n_lat, n_lon, foot, dep, cmap, adj_hbm, wlon_hbm, wlat_hbm, out_hbm,
    prof, tag, send, recv, state, later, wlon, wlat, edge_out, edge_in,
    load_sem, out_sem, send_sem, recv_sem, edge_send_sem, edge_recv_sem,
):
    lat, lon = lax.axis_index("lat"), lax.axis_index("lon")
    n_dev = n_lat * n_lon
    rows, levels, cols = state.shape
    obs = dep.shape[0]
    slots = recv.shape[2]

    barrier = pltpu.get_barrier_semaphore()

    def greet(i, carry):
        pl.semaphore_signal(
            barrier, inc=1,
            device_id=((lat + i // n_lon) % n_lat, (lon + i % n_lon) % n_lon),
            device_id_type=MESH,
        )
        return carry

    lax.fori_loop(1, n_dev, greet, 0)

    def load(r, carry):
        pltpu.make_async_copy(adj_hbm.at[:, r, :], state.at[r], load_sem.at[0]).start()
        pltpu.make_async_copy(wlon_hbm.at[:, r, :], wlon.at[r], load_sem.at[1]).start()
        pltpu.make_async_copy(wlat_hbm.at[:, r, :], wlat.at[r], load_sem.at[2]).start()
        return carry

    lax.fori_loop(0, rows, load, 0)

    shift_grid, shift_row, shift_col = log2(n_lon * cols), log2(rows), log2(cols)
    cells = foot[...]
    grid_row = lax.shift_right_logical(cells, shift_grid)
    grid_col = cells & (n_lon * cols - 1)
    owner = (
        lax.shift_right_logical(grid_row[0:1], shift_row) * n_lon
        + lax.shift_right_logical(grid_col[0:1], shift_col)
    )
    in_row = grid_row & (rows - 1)
    in_col = grid_col & (cols - 1)

    def base(cell):
        low = jnp.minimum(jnp.minimum(cell[0:1], cell[1:2]), jnp.minimum(cell[2:3], cell[3:4]))
        high = jnp.maximum(jnp.maximum(cell[0:1], cell[1:2]), jnp.maximum(cell[2:3], cell[3:4]))
        return jnp.where(high - low == 1, low, high)

    base_row, base_col = base(in_row), base(in_col)
    chunk = 256
    upper = jnp.where(
        lax.broadcasted_iota(jnp.int32, (chunk, chunk), 0)
        <= lax.broadcasted_iota(jnp.int32, (chunk, chunk), 1),
        1.0, 0.0,
    ).astype(jnp.bfloat16)
    owners = lax.broadcasted_iota(jnp.int32, (n_dev, chunk), 0)
    seen = jnp.zeros((n_dev, 1), jnp.float32)
    for start in range(0, obs, chunk):
        hot = jnp.where(owners == owner[:, start:start + chunk], 1.0, 0.0)
        count = jnp.dot(hot.astype(jnp.bfloat16), upper, preferred_element_type=jnp.float32) + seen
        place = jnp.sum(hot * count, axis=0, keepdims=True) - 1.0
        seen = count[:, chunk - 1:chunk]
        tag[0:1, start:start + chunk] = place.astype(jnp.int32)
    tag[1:2, :] = owner

    prof[0:levels, :] = nt_dot(cmap[...], dep[...]).astype(jnp.bfloat16)
    which = lax.broadcasted_iota(jnp.int32, (META, obs), 0)
    prof[levels:levels + META, :] = jnp.where(
        which == 0, base_row, jnp.where(which == 1, base_col, 0)
    ).astype(jnp.float32).astype(jnp.bfloat16)

    pl.semaphore_wait(barrier, n_dev - 1)

    def away(k):
        step = (k + 1) // 2
        return (n_lon // 2 + n_lon + step * (1 - 2 * (k % 2))) % n_lon

    def transfer(i, a, k):
        return pltpu.make_async_remote_copy(
            src_ref=send.at[i], dst_ref=recv.at[i],
            send_sem=send_sem.at[i], recv_sem=recv_sem.at[i],
            device_id=((lat + a) % n_lat, (lon + away(k)) % n_lon),
            device_id_type=MESH,
        )

    def route(k, carry):
        place, owner = tag[0:1, :], tag[1:2, :]
        slot = lax.broadcasted_iota(jnp.int32, (slots, obs), 0)
        hots = []
        for a in range(n_lat):
            target = (lat + a) % n_lat * n_lon + (lon + away(k)) % n_lon
            wanted = jnp.where(owner == target, place, -1)
            hots.append(jnp.where(slot == wanted, 1.0, 0.0).astype(jnp.bfloat16))
        blocks = nt_dot(prof[...], jnp.concatenate(hots, axis=0)).astype(jnp.bfloat16)
        for a in range(n_lat):
            i = k * n_lat + a
            block = blocks[:, a * slots:(a + 1) * slots]
            if a == 0:
                @pl.when(k == n_lon - 1)
                def _():
                    recv[i] = block

                @pl.when(k < n_lon - 1)
                def _():
                    send[i] = block
                    transfer(i, a, k).start()
            else:
                send[i] = block
                transfer(i, a, k).start()
        return carry

    lax.fori_loop(0, n_lon, route, 0)

    for which, buf in enumerate((state, wlon, wlat)):
        pltpu.make_async_copy(buf, buf, load_sem.at[which]).wait()

    tile = 8
    depth = n_lat * slots

    def deposit(k, carry):
        for a in range(n_lat):
            if a == 0:
                @pl.when(k < n_lon - 1)
                def _():
                    transfer(k * n_lat, 0, k).wait_recv()
            else:
                transfer(k * n_lat + a, a, k).wait_recv()
        parts = [recv[k * n_lat + a] for a in range(n_lat)]
        got = jnp.concatenate([p[0:levels] for p in parts], axis=1)
        meta = jnp.concatenate([p[levels:levels + META] for p in parts], axis=1)
        meta = meta.astype(jnp.float32).astype(jnp.int32)
        at_row, at_col = meta[0:1], meta[1:2]
        col = lax.broadcasted_iota(jnp.int32, (cols, depth), 0)
        col_hot = jnp.where(
            (col == at_col) | (col == ((at_col + 1) & (cols - 1))), 0.25, 0.0
        ).astype(jnp.bfloat16)
        next_row = (at_row + 1) & (rows - 1)
        stacked = got.reshape(levels // 16, 16, depth)

        def rows_of(t, carry):
            lhs = []
            for j in range(tile):
                r = t * tile + j
                hot = jnp.where((at_row == r) | (next_row == r), 1.0, 0.0)
                hot = jnp.broadcast_to(hot, (16, depth)).astype(jnp.bfloat16)
                lhs.append((stacked * hot[None]).reshape(levels, depth))
            out = nt_dot(jnp.concatenate(lhs, axis=0), col_hot)
            at = pl.ds(t * tile, tile)
            state[at] = state[at] + out.reshape(tile, levels, cols)
            return carry

        lax.fori_loop(0, rows // tile, rows_of, 0)
        return carry

    lax.fori_loop(0, n_lon, deposit, 0)

    part = 32
    lane = lax.broadcasted_iota(jnp.int32, (part, cols), 1)
    west, east = (lon + n_lon - 1) % n_lon, (lon + 1) % n_lon
    south, north = (lat + n_lat - 1) % n_lat, (lat + 1) % n_lat
    targets = ((lat, west), (lat, east), (south, lon), (north, lon))

    def edge_copy(step, side):
        return pltpu.make_async_remote_copy(
            src_ref=edge_out.at[step, side], dst_ref=edge_in.at[step, side],
            send_sem=edge_send_sem.at[step, side], recv_sem=edge_recv_sem.at[step, side],
            device_id=targets[side], device_id_type=MESH,
        )

    def split(s, w):
        flux = (0.5 * w) * s
        even = RATE * s
        return even + flux, even - flux

    for step in range(STEPS):
        src, dst = (state, later) if step % 2 == 0 else (later, state)

        edge_out[step, 2] = split(src[0], wlat[0])[0]
        edge_copy(step, 2).start()
        edge_out[step, 3] = split(src[rows - 1], wlat[rows - 1])[1]
        edge_copy(step, 3).start()

        def pack(q, carry):
            at = pl.ds(pl.multiple_of(q * part, part), part)

            def one(r, packed):
                plus, minus = split(src[r, at, :], wlon[r, at, :])
                return (
                    jnp.where(lane == r, pltpu.roll(plus, r, 1), packed[0]),
                    jnp.where(lane == r, pltpu.roll(minus, r + 1, 1), packed[1]),
                )

            zero = jnp.zeros((part, cols), jnp.float32)
            packed = lax.fori_loop(0, rows, one, (zero, zero))
            edge_out[step, 0, at, :] = packed[0]
            edge_out[step, 1, at, :] = packed[1]
            return carry

        lax.fori_loop(0, levels // part, pack, 0)
        edge_copy(step, 0).start()
        edge_copy(step, 1).start()

        def inner(r, carry):
            above, below = jnp.minimum(r + 1, rows - 1), jnp.maximum(r - 1, 0)
            for q in range(levels // part):
                at = pl.ds(q * part, part)
                s = src[r, at, :]
                plus, minus = split(s, wlon[r, at, :])
                from_north = split(src[above, at, :], wlat[above, at, :])[0]
                from_south = split(src[below, at, :], wlat[below, at, :])[1]
                dst[r, at, :] = (
                    (1.0 - 4.0 * RATE) * s
                    + jnp.where(lane == cols - 1, 0.0, pltpu.roll(plus, cols - 1, 1))
                    + jnp.where(lane == 0, 0.0, pltpu.roll(minus, 1, 1))
                    + jnp.where(r < rows - 1, from_north, 0.0)
                    + jnp.where(r > 0, from_south, 0.0)
                )
            return carry

        lax.fori_loop(0, rows, inner, 0)

        edge_copy(step, 2).wait()
        edge_copy(step, 3).wait()
        dst[rows - 1] = dst[rows - 1] + jnp.where(lat < n_lat - 1, edge_in[step, 2], 0.0)
        dst[0] = dst[0] + jnp.where(lat > 0, edge_in[step, 3], 0.0)
        edge_copy(step, 0).wait()
        edge_copy(step, 1).wait()
        last = step == STEPS - 1

        def mend(r, carry):
            for q in range(levels // part):
                at = pl.ds(q * part, part)
                from_east = pltpu.roll(edge_in[step, 0, at, :], cols - 1 - r, 1)
                from_west = pltpu.roll(edge_in[step, 1, at, :], (cols - r) % cols, 1)
                dst[r, at, :] = dst[r, at, :] + jnp.where(
                    lane == cols - 1, from_east, jnp.where(lane == 0, from_west, 0.0)
                )
            if last:
                pltpu.make_async_copy(dst.at[r], out_hbm.at[:, r, :], out_sem).start()
            return carry

        lax.fori_loop(0, rows, mend, 0)

    final = state if STEPS % 2 == 0 else later
    pltpu.make_async_copy(final, final, out_sem).wait()

    def drain(i, carry):
        @pl.when(i != (n_lon - 1) * n_lat)
        def _():
            pltpu.make_async_remote_copy(
                src_ref=send.at[i], dst_ref=recv.at[i],
                send_sem=send_sem.at[i], recv_sem=recv_sem.at[i],
                device_id=(north, lon), device_id_type=MESH,
            ).wait_send()
        return carry

    lax.fori_loop(0, n_dev, drain, 0)


def local(departures, footprint, channel_map, adjoint_in, wind_lon, wind_lat):
    n_lat, n_lon = lax.axis_size("lat"), lax.axis_size("lon")
    n_dev = n_lat * n_lon
    levels, rows, cols = adjoint_in.shape
    obs = departures.shape[0]
    capacity = 2 * obs // n_dev
    slots = -(-capacity // LANES) * LANES
    block = (n_dev, levels + META, slots)
    field = pltpu.VMEM((rows, levels, cols), jnp.float32)
    vmem, anywhere = pl.BlockSpec(memory_space=pltpu.VMEM), pl.BlockSpec(memory_space=pl.ANY)
    return pl.pallas_call(
        functools.partial(kernel, n_lat, n_lon),
        out_shape=jax.ShapeDtypeStruct(adjoint_in.shape, jnp.float32),
        in_specs=[vmem] * 3 + [anywhere] * 3,
        out_specs=anywhere,
        scratch_shapes=[
            pltpu.VMEM((levels + META, obs), jnp.bfloat16),
            pltpu.VMEM((8, obs), jnp.int32),
            pltpu.VMEM(block, jnp.bfloat16),
            pltpu.VMEM(block, jnp.bfloat16),
            field, field, field, field,
            pltpu.VMEM((STEPS, 4, levels, cols), jnp.float32),
            pltpu.VMEM((STEPS, 4, levels, cols), jnp.float32),
            pltpu.SemaphoreType.DMA((3,)),
            pltpu.SemaphoreType.DMA,
            pltpu.SemaphoreType.DMA((n_dev,)),
            pltpu.SemaphoreType.DMA((n_dev,)),
            pltpu.SemaphoreType.DMA((STEPS, 4)),
            pltpu.SemaphoreType.DMA((STEPS, 4)),
        ],
        compiler_params=pltpu.CompilerParams(
            collective_id=0, has_side_effects=True, vmem_limit_bytes=48 << 20
        ),
        name="assimilate",
    )(footprint.T, departures, channel_map.T, adjoint_in, wind_lon, wind_lat)


def solution(mesh):
    in_specs = (
        P(("lat", "lon"), None),
        P(("lat", "lon"), None),
        P(),
        P(None, "lat", "lon"),
        P(None, "lat", "lon"),
        P(None, "lat", "lon"),
    )
    out_specs = P(None, "lat", "lon")
    return jax.shard_map(local, mesh=mesh, in_specs=in_specs, out_specs=out_specs, check_vma=False)
```

profile of v0, /device:TPU:0, one launch (start us, length us, event | category | flops | bytes accessed | tf_op | source)
XLA Modules:
  0.0 87.3 jit_solution(14116318194067723902)
XLA Ops:
  0.0 0.9 %copy.7 = bf16[256,128]{0,1:T(8,128)(2,1)S(1)} copy(bf16[256,128]{1,0:T(8,128)(2,1)} %param.8) | data formatting | bytes 131072 | tf_op args[2]
  0.9 0.0 copy-start
  1.0 1.6 %copy-done = f32[128,32,128]{2,1,0:T(8,128)S(1)} copy-done((f32[128,32,128]{2,1,0:T(8,128)S(1)}, f32[128,32,128]{2,1,0:T(8,128)}, u32[]{:S(2)}) %copy-start) | copy-done | bytes 2097176
  2.5 0.0 copy-start.1
  2.5 1.2 %copy-done.1 = bf16[2048,256]{1,0:T(8,128)(2,1)S(1)} copy-done((bf16[2048,256]{1,0:T(8,128)(2,1)S(1)}, bf16[2048,256]{1,0:T(8,128)(2,1)}, u32[]{:S(2)}) %copy-start.1) | copy-done | bytes 1048600
  3.8 0.0 copy-start.2
  3.8 0.8 copy-done.2
  4.5 81.5 %assimilate.1 = f32[128,32,128]{2,1,0:T(8,128)S(1)} custom-call(s32[4,2048]{1,0:T(4,128)S(1)} %bitcast.3, bf16[2048,256]{1,0:T(8,128)(2,1)S(1)} %copy-done.1, bf16[128,256]{1,0:T(8,128)(2,1)S(1)} %bitcast.2, f32[128,32,128]{2,1,0:T(8,128)S(1)} %copy-done, f32[128,32,128]{2,1,0:T(8,128)} %wlon_hbm.1, f32[128,32,128]{2,1,0:T(8,128)} %wlat_hbm.1), custom_call_target="tpu_custom_call" | custom-call | tf_op jit(solution)/shard_map/assimilate/pallas_call | solution.py:294
  86.0 1.3 %copy.9 = f32[128,32,128]{2,1,0:T(8,128)} copy(f32[128,32,128]{2,1,0:T(8,128)S(1)} %assimilate.1) | data formatting | bytes 4194304
Async XLA Ops:
  0.9 1.6 %copy-start = (f32[128,32,128]{2,1,0:T(8,128)S(1)}, f32[128,32,128]{2,1,0:T(8,128)}, u32[]{:S(2)}) copy-start(f32[128,32,128]{2,1,0:T(8,128)} %adj_hbm.1) | copy-start | bytes 6291460
  2.5 1.2 %copy-start.1 = (bf16[2048,256]{1,0:T(8,128)(2,1)S(1)}, bf16[2048,256]{1,0:T(8,128)(2,1)}, u32[]{:S(2)}) copy-start(bf16[2048,256]{1,0:T(8,128)(2,1)} %dep.1) | copy-start | bytes 3145732
  3.8 0.8 copy-start.2
where the time goes:
time: 87.6 us; the launch traced here: 87.3 us
  Pallas kernels  81.5 us (93%)
  local copies, waits for them, and re-layouts  5.83 us (7%)
    pallas_call x1, Pallas kernels, local(): pl.pallas_call(functools.partial(kernel, n_lat, n_lon), out_shape=jax.Sha...  81.5 us
    unnamed x8, local copies, waits for them, and re-layouts  5.83 us

commit v1 on v0

--- a/solution.py
+++ b/solution.py
@@ -24,8 +24,8 @@
 
 
 def kernel(
-    n_lat, n_lon, foot, dep, cmap, adj_hbm, wlon_hbm, wlat_hbm, out_hbm,
-    prof, tag, send, recv, state, later, wlon, wlat, edge_out, edge_in,
+    n_lat, n_lon, foot, dep_hbm, cmap, adj_hbm, wlon_hbm, wlat_hbm, out_hbm,
+    dep, prof, tag, send, recv, state, later, wlon, wlat, edge_out, edge_in,
     load_sem, out_sem, send_sem, recv_sem, edge_send_sem, edge_recv_sem,
 ):
     lat, lon = lax.axis_index("lat"), lax.axis_index("lon")
@@ -45,6 +45,8 @@
         return carry
 
     lax.fori_loop(1, n_dev, greet, 0)
+
+    pltpu.make_async_copy(dep_hbm, dep, load_sem.at[3]).start()
 
     def load(r, carry):
         pltpu.make_async_copy(adj_hbm.at[:, r, :], state.at[r], load_sem.at[0]).start()
@@ -87,7 +89,10 @@
         tag[0:1, start:start + chunk] = place.astype(jnp.int32)
     tag[1:2, :] = owner
 
-    prof[0:levels, :] = nt_dot(cmap[...], dep[...]).astype(jnp.bfloat16)
+    pltpu.make_async_copy(dep_hbm, dep, load_sem.at[3]).wait()
+    prof[0:levels, :] = lax.dot_general(
+        cmap[...], dep[...], (((0,), (1,)), ((), ())), preferred_element_type=jnp.float32
+    ).astype(jnp.bfloat16)
     which = lax.broadcasted_iota(jnp.int32, (META, obs), 0)
     prof[levels:levels + META, :] = jnp.where(
         which == 0, base_row, jnp.where(which == 1, base_col, 0)
@@ -95,7 +100,13 @@
 
     pl.semaphore_wait(barrier, n_dev - 1)
 
+    def place_of(k):
+        return k // 2 + (k % 2) * (n_lon - 1 - 2 * (k // 2))
+
+    own = 1
+
     def away(k):
+        k = place_of(k)
         step = (k + 1) // 2
         return (n_lon // 2 + n_lon + step * (1 - 2 * (k % 2))) % n_lon
 
@@ -120,11 +131,11 @@
             i = k * n_lat + a
             block = blocks[:, a * slots:(a + 1) * slots]
             if a == 0:
-                @pl.when(k == n_lon - 1)
+                @pl.when(k == own)
                 def _():
                     recv[i] = block
 
-                @pl.when(k < n_lon - 1)
+                @pl.when(k != own)
                 def _():
                     send[i] = block
                     transfer(i, a, k).start()
@@ -135,6 +146,7 @@
 
     lax.fori_loop(0, n_lon, route, 0)
 
+    later[...] = jnp.zeros_like(later)
     for which, buf in enumerate((state, wlon, wlat)):
         pltpu.make_async_copy(buf, buf, load_sem.at[which]).wait()
 
@@ -144,7 +156,7 @@
     def deposit(k, carry):
         for a in range(n_lat):
             if a == 0:
-                @pl.when(k < n_lon - 1)
+                @pl.when(k != own)
                 def _():
                     transfer(k * n_lat, 0, k).wait_recv()
             else:
@@ -154,39 +166,45 @@
         meta = jnp.concatenate([p[levels:levels + META] for p in parts], axis=1)
         meta = meta.astype(jnp.float32).astype(jnp.int32)
         at_row, at_col = meta[0:1], meta[1:2]
-        col = lax.broadcasted_iota(jnp.int32, (cols, depth), 0)
-        col_hot = jnp.where(
-            (col == at_col) | (col == ((at_col + 1) & (cols - 1))), 0.25, 0.0
+        cell = lax.broadcasted_iota(jnp.int32, (2 * cols, depth), 0)
+        first = at_row % 2 * cols
+        cell_hot = jnp.where(
+            (cell == first + at_col) | (cell == first + ((at_col + 1) & (cols - 1))), 0.25, 0.0
         ).astype(jnp.bfloat16)
-        next_row = (at_row + 1) & (rows - 1)
+        pair = lax.shift_right_logical(at_row, 1)
         stacked = got.reshape(levels // 16, 16, depth)
 
         def rows_of(t, carry):
             lhs = []
             for j in range(tile):
-                r = t * tile + j
-                hot = jnp.where((at_row == r) | (next_row == r), 1.0, 0.0)
+                hot = jnp.where(pair == t * tile + j, 1.0, 0.0)
                 hot = jnp.broadcast_to(hot, (16, depth)).astype(jnp.bfloat16)
                 lhs.append((stacked * hot[None]).reshape(levels, depth))
-            out = nt_dot(jnp.concatenate(lhs, axis=0), col_hot)
-            at = pl.ds(t * tile, tile)
-            state[at] = state[at] + out.reshape(tile, levels, cols)
+            out = nt_dot(jnp.concatenate(lhs, axis=0), cell_hot)
+            for j in range(tile):
+                r = 2 * (t * tile + j)
+                here = out[j * levels:(j + 1) * levels]
+                later[r] = later[r] + here[:, 0:cols]
+                later[r + 1] = later[r + 1] + here[:, cols:2 * cols]
             return carry
 
-        lax.fori_loop(0, rows // tile, rows_of, 0)
+        lax.fori_loop(0, rows // 2 // tile, rows_of, 0)
         return carry
 
     lax.fori_loop(0, n_lon, deposit, 0)
 
-    part = 32
+    part = 16
+    assert 2 * rows <= cols and rows % 4 == 0
     lane = lax.broadcasted_iota(jnp.int32, (part, cols), 1)
+    all_lane = lax.broadcasted_iota(jnp.int32, (levels, cols), 1)
+    side_half = jnp.where(lane == cols - 1, -0.5, 0.5)
     west, east = (lon + n_lon - 1) % n_lon, (lon + 1) % n_lon
     south, north = (lat + n_lat - 1) % n_lat, (lat + 1) % n_lat
     targets = ((lat, west), (lat, east), (south, lon), (north, lon))
 
     def edge_copy(step, side):
         return pltpu.make_async_remote_copy(
-            src_ref=edge_out.at[step, side], dst_ref=edge_in.at[step, side],
+            src_ref=edge_out.at[step, max(side, 1)], dst_ref=edge_in.at[step, side],
             send_sem=edge_send_sem.at[step, side], recv_sem=edge_recv_sem.at[step, side],
             device_id=targets[side], device_id_type=MESH,
         )
@@ -196,80 +214,116 @@
         even = RATE * s
         return even + flux, even - flux
 
+    def pack_row(packed, r, s, w):
+        side = (RATE + side_half * w) * s
+        if r > 0:
+            side = pltpu.roll(side, 2 * r, 1)
+        return jnp.where((lane == 2 * r) | (lane == (2 * r - 1) % cols), side, packed)
+
+    def part_at(q):
+        return pl.ds(pl.multiple_of(q * part, part), part)
+
+    def pack(q, carry):
+        at = part_at(q)
+        packed = jnp.zeros((part, cols), jnp.float32)
+        below = later[rows - 1, at, :]
+        for r in range(rows):
+            here = later[r, at, :]
+            s = state[r, at, :] + (here + below)
+            state[r, at, :] = s
+            packed = pack_row(packed, r, s, wlon[r, at, :])
+            below = here
+        edge_out[0, 1, at, :] = packed
+        return carry
+
+    lax.fori_loop(0, levels // part, pack, 0)
+    edge_copy(0, 0).start()
+    edge_copy(0, 1).start()
+    edge_out[0, 2] = split(state[0], wlat[0])[0]
+    edge_out[0, 3] = split(state[rows - 1], wlat[rows - 1])[1]
+    edge_copy(0, 2).start()
+    edge_copy(0, 3).start()
+
     for step in range(STEPS):
         src, dst = (state, later) if step % 2 == 0 else (later, state)
-
-        edge_out[step, 2] = split(src[0], wlat[0])[0]
-        edge_copy(step, 2).start()
-        edge_out[step, 3] = split(src[rows - 1], wlat[rows - 1])[1]
-        edge_copy(step, 3).start()
-
-        def pack(q, carry):
-            at = pl.ds(pl.multiple_of(q * part, part), part)
-
-            def one(r, packed):
-                plus, minus = split(src[r, at, :], wlon[r, at, :])
-                return (
-                    jnp.where(lane == r, pltpu.roll(plus, r, 1), packed[0]),
-                    jnp.where(lane == r, pltpu.roll(minus, r + 1, 1), packed[1]),
-                )
-
-            zero = jnp.zeros((part, cols), jnp.float32)
-            packed = lax.fori_loop(0, rows, one, (zero, zero))
-            edge_out[step, 0, at, :] = packed[0]
-            edge_out[step, 1, at, :] = packed[1]
+        last = step == STEPS - 1
+
+        def inner(q, carry):
+            at = part_at(q)
+            centre = below = None
+            for r in range(rows + 1):
+                above = None
+                if r < rows:
+                    s = src[r, at, :]
+                    plus, minus = split(s, wlon[r, at, :])
+                    across = (
+                        (1.0 - 4.0 * RATE) * s
+                        + jnp.where(lane == cols - 1, 0.0, pltpu.roll(plus, cols - 1, 1))
+                        + jnp.where(lane == 0, 0.0, pltpu.roll(minus, 1, 1))
+                    )
+                    above, here = split(s, wlat[r, at, :])
+                if r > 0:
+                    total = centre
+                    if above is not None:
+                        total = total + above
+                    dst[r - 1, at, :] = total
+                if r < rows:
+                    centre = across if below is None else across + below
+                    below = here
             return carry
 
-        lax.fori_loop(0, levels // part, pack, 0)
-        edge_copy(step, 0).start()
-        edge_copy(step, 1).start()
-
-        def inner(r, carry):
-            above, below = jnp.minimum(r + 1, rows - 1), jnp.maximum(r - 1, 0)
-            for q in range(levels // part):
-                at = pl.ds(q * part, part)
-                s = src[r, at, :]
-                plus, minus = split(s, wlon[r, at, :])
-                from_north = split(src[above, at, :], wlat[above, at, :])[0]
-                from_south = split(src[below, at, :], wlat[below, at, :])[1]
-                dst[r, at, :] = (
-                    (1.0 - 4.0 * RATE) * s
-                    + jnp.where(lane == cols - 1, 0.0, pltpu.roll(plus, cols - 1, 1))
-                    + jnp.where(lane == 0, 0.0, pltpu.roll(minus, 1, 1))
-                    + jnp.where(r < rows - 1, from_north, 0.0)
-                    + jnp.where(r > 0, from_south, 0.0)
-                )
-            return carry
-
-        lax.fori_loop(0, rows, inner, 0)
-
-        edge_copy(step, 2).wait()
-        edge_copy(step, 3).wait()
-        dst[rows - 1] = dst[rows - 1] + jnp.where(lat < n_lat - 1, edge_in[step, 2], 0.0)
-        dst[0] = dst[0] + jnp.where(lat > 0, edge_in[step, 3], 0.0)
-        edge_copy(step, 0).wait()
-        edge_copy(step, 1).wait()
-        last = step == STEPS - 1
-
-        def mend(r, carry):
-            for q in range(levels // part):
-                at = pl.ds(q * part, part)
-                from_east = pltpu.roll(edge_in[step, 0, at, :], cols - 1 - r, 1)
-                from_west = pltpu.roll(edge_in[step, 1, at, :], (cols - r) % cols, 1)
-                dst[r, at, :] = dst[r, at, :] + jnp.where(
-                    lane == cols - 1, from_east, jnp.where(lane == 0, from_west, 0.0)
-                )
-            if last:
-                pltpu.make_async_copy(dst.at[r], out_hbm.at[:, r, :], out_sem).start()
-            return carry
-
-        lax.fori_loop(0, rows, mend, 0)
+        lax.fori_loop(0, levels // part, inner, 0)
+
+        for side in range(4):
+            edge_copy(step, side).wait()
+        from_north = jnp.where(lat < n_lat - 1, edge_in[step, 2], 0.0)
+        from_south = jnp.where(lat > 0, edge_in[step, 3], 0.0)
+        dst[rows - 1] = dst[rows - 1] + from_north
+        dst[0] = dst[0] + from_south
+        edge_in[step, 0] = jnp.where(
+            all_lane % 2 == 0, edge_in[step, 0], pltpu.roll(edge_in[step, 1], 2, 1)
+        )
+
+        if not last:
+            def mend(q, carry):
+                at = part_at(q)
+                packed = jnp.zeros((part, cols), jnp.float32)
+                both = edge_in[step, 0, at, :]
+                for r in range(rows):
+                    moved = pltpu.roll(both, cols - 1 - 2 * r, 1)
+                    s = dst[r, at, :] + jnp.where((lane == cols - 1) | (lane == 0), moved, 0.0)
+                    dst[r, at, :] = s
+                    packed = pack_row(packed, r, s, wlon[r, at, :])
+                edge_out[step + 1, 1, at, :] = packed
+                return carry
+
+            lax.fori_loop(0, levels // part, mend, 0)
+            edge_copy(step + 1, 0).start()
+            edge_copy(step + 1, 1).start()
+            edge_out[step + 1, 2] = split(dst[0], wlat[0])[0]
+            edge_out[step + 1, 3] = split(dst[rows - 1], wlat[rows - 1])[1]
+            edge_copy(step + 1, 2).start()
+            edge_copy(step + 1, 3).start()
+        else:
+            def finish(t, carry):
+                for j in range(4):
+                    r = t * 4 + j
+                    for q in range(levels // part):
+                        at = pl.ds(q * part, part)
+                        moved = pltpu.roll(edge_in[step, 0, at, :], cols - 1 - 2 * r, 1)
+                        dst[r, at, :] = dst[r, at, :] + jnp.where(
+                            (lane == cols - 1) | (lane == 0), moved, 0.0
+                        )
+                    pltpu.make_async_copy(dst.at[r], out_hbm.at[:, r, :], out_sem).start()
+                return carry
+
+            lax.fori_loop(0, rows // 4, finish, 0)
 
     final = state if STEPS % 2 == 0 else later
     pltpu.make_async_copy(final, final, out_sem).wait()
 
     def drain(i, carry):
-        @pl.when(i != (n_lon - 1) * n_lat)
+        @pl.when(i != own * n_lat)
         def _():
             pltpu.make_async_remote_copy(
                 src_ref=send.at[i], dst_ref=recv.at[i],
@@ -291,12 +345,14 @@
     block = (n_dev, levels + META, slots)
     field = pltpu.VMEM((rows, levels, cols), jnp.float32)
     vmem, anywhere = pl.BlockSpec(memory_space=pltpu.VMEM), pl.BlockSpec(memory_space=pl.ANY)
+    hbm = pl.BlockSpec(memory_space=pltpu.HBM)
     return pl.pallas_call(
         functools.partial(kernel, n_lat, n_lon),
         out_shape=jax.ShapeDtypeStruct(adjoint_in.shape, jnp.float32),
-        in_specs=[vmem] * 3 + [anywhere] * 3,
+        in_specs=[vmem, hbm, vmem] + [hbm] * 3,
         out_specs=anywhere,
         scratch_shapes=[
+            pltpu.VMEM(departures.shape, jnp.bfloat16),
             pltpu.VMEM((levels + META, obs), jnp.bfloat16),
             pltpu.VMEM((8, obs), jnp.int32),
             pltpu.VMEM(block, jnp.bfloat16),
@@ -304,7 +360,7 @@
             field, field, field, field,
             pltpu.VMEM((STEPS, 4, levels, cols), jnp.float32),
             pltpu.VMEM((STEPS, 4, levels, cols), jnp.float32),
-            pltpu.SemaphoreType.DMA((3,)),
+            pltpu.SemaphoreType.DMA((4,)),
             pltpu.SemaphoreType.DMA,
             pltpu.SemaphoreType.DMA((n_dev,)),
             pltpu.SemaphoreType.DMA((n_dev,)),
@@ -312,10 +368,10 @@
             pltpu.SemaphoreType.DMA((STEPS, 4)),
         ],
         compiler_params=pltpu.CompilerParams(
-            collective_id=0, has_side_effects=True, vmem_limit_bytes=48 << 20
+            collective_id=0, has_side_effects=True, vmem_limit_bytes=62 << 20
         ),
         name="assimilate",
-    )(footprint.T, departures, channel_map.T, adjoint_in, wind_lon, wind_lat)
+    )(footprint.T, departures, channel_map, adjoint_in, wind_lon, wind_lat)
 
 
 def solution(mesh):

time: 87.6 us -> 56.1 us (0.64)
  Pallas kernels: 81.5 us -> 52.8 us
  local copies, waits for them, and re-layouts: 5.83 us -> 3.08 us
    pallas_call x1, Pallas kernels: 81.5 us -> 52.8 us  [local(): pl.pallas_call(functools.partial(kernel, n_lat, n_lon), out_shape=jax.Sha...]
    unnamed x8 -> x1, local copies, waits for them, and re-layouts: 5.83 us -> 3.08 us
where the time goes in v1:
time: 56.1 us; the launch traced here: 55.9 us
  Pallas kernels  52.8 us (94%)
  local copies, waits for them, and re-layouts  3.08 us (5%)
    pallas_call x1, Pallas kernels, local(): pl.pallas_call(functools.partial(kernel, n_lat, n_lon), out_shape=jax.Sha...  52.8 us
    unnamed x1, local copies, waits for them, and re-layouts  3.08 us

profile of v1, /device:TPU:0, one launch (start us, length us, event | category | flops | bytes accessed | tf_op | source)
XLA Modules:
  0.0 55.9 jit_solution(1949520561643811970)
XLA Ops:
  0.0 52.8 %assimilate.1 = f32[128,32,128]{2,1,0:T(8,128)} custom-call(s32[4,2048]{1,0:T(4,128)} %bitcast.1, bf16[2048,256]{1,0:T(8,128)(2,1)} %dep_hbm.1, bf16[256,128]{1,0:T(8,128)(2,1)} %cmap.1, f32[128,32,128]{2,1,0:T(8,128)} %adj_hbm.1, f32[128,32,128]{2,1,0:T(8,128)} %wlon_hbm.1, f32[128,32,128]{2,1,0:T(8,128)} %wlat_hbm.1), custom_call_target="tpu_custom_call" | custom-call | tf_op jit(solution)/shard_map/assimilate/pallas_call | solution.py:349
  52.8 3.1 %copy.8 = f32[128,32,128]{2,1,0:T(8,128)} copy(f32[128,32,128]{2,1,0:T(8,128)} %assimilate.1) | data formatting | bytes 4194304

commit v2 on v1

--- a/solution.py
+++ b/solution.py
@@ -10,7 +10,7 @@
 STEPS = 2
 RATE = 0.2
 LANES = 128
-META = 16
+META = 8
 MESH = pl.DeviceIdType.MESH
 
 
@@ -25,7 +25,7 @@
 
 def kernel(
     n_lat, n_lon, foot, dep_hbm, cmap, adj_hbm, wlon_hbm, wlat_hbm, out_hbm,
-    dep, prof, tag, send, recv, state, later, wlon, wlat, edge_out, edge_in,
+    dep, prof, tag, send, recv, state, later, wlon, wlat, edge_out, edge_in, fringe,
     load_sem, out_sem, send_sem, recv_sem, edge_send_sem, edge_recv_sem,
 ):
     lat, lon = lax.axis_index("lat"), lax.axis_index("lon")
@@ -233,16 +233,40 @@
             state[r, at, :] = s
             packed = pack_row(packed, r, s, wlon[r, at, :])
             below = here
-        edge_out[0, 1, at, :] = packed
-        return carry
-
+        edge_out[0, 1, at, :] = packed.astype(jnp.bfloat16)
+        return carry
+
+    def send_rows(step, first, final):
+        edge_out[step, 2] = split(first, wlat[0])[0].astype(jnp.bfloat16)
+        edge_out[step, 3] = split(final, wlat[rows - 1])[1].astype(jnp.bfloat16)
+
+        @pl.when(lat > 0)
+        def _():
+            edge_copy(step, 2).start()
+
+        @pl.when(lat < n_lat - 1)
+        def _():
+            edge_copy(step, 3).start()
+
+    def await_rows(step):
+        @pl.when(lat > 0)
+        def _():
+            edge_copy(step, 2).wait_send()
+            edge_copy(step, 3).wait_recv()
+
+        @pl.when(lat < n_lat - 1)
+        def _():
+            edge_copy(step, 3).wait_send()
+            edge_copy(step, 2).wait_recv()
+
+    send_rows(
+        0,
+        state[0] + (later[0] + later[rows - 1]),
+        state[rows - 1] + (later[rows - 1] + later[rows - 2]),
+    )
     lax.fori_loop(0, levels // part, pack, 0)
     edge_copy(0, 0).start()
     edge_copy(0, 1).start()
-    edge_out[0, 2] = split(state[0], wlat[0])[0]
-    edge_out[0, 3] = split(state[rows - 1], wlat[rows - 1])[1]
-    edge_copy(0, 2).start()
-    edge_copy(0, 3).start()
 
     for step in range(STEPS):
         src, dst = (state, later) if step % 2 == 0 else (later, state)
@@ -274,43 +298,55 @@
 
         lax.fori_loop(0, levels // part, inner, 0)
 
-        for side in range(4):
-            edge_copy(step, side).wait()
-        from_north = jnp.where(lat < n_lat - 1, edge_in[step, 2], 0.0)
-        from_south = jnp.where(lat > 0, edge_in[step, 3], 0.0)
-        dst[rows - 1] = dst[rows - 1] + from_north
-        dst[0] = dst[0] + from_south
-        edge_in[step, 0] = jnp.where(
-            all_lane % 2 == 0, edge_in[step, 0], pltpu.roll(edge_in[step, 1], 2, 1)
+        await_rows(step)
+
+        @pl.when(lat < n_lat - 1)
+        def _():
+            dst[rows - 1] = dst[rows - 1] + edge_in[step, 2].astype(jnp.float32)
+
+        @pl.when(lat > 0)
+        def _():
+            dst[0] = dst[0] + edge_in[step, 3].astype(jnp.float32)
+
+        edge_copy(step, 0).wait()
+        edge_copy(step, 1).wait()
+        both = jnp.where(
+            all_lane % 2 == 0,
+            edge_in[step, 0].astype(jnp.float32),
+            pltpu.roll(edge_in[step, 1].astype(jnp.float32), 2, 1),
         )
+        fringe[...] = both
+        at_side = (all_lane == cols - 1) | (all_lane == 0)
 
         if not last:
             def mend(q, carry):
                 at = part_at(q)
                 packed = jnp.zeros((part, cols), jnp.float32)
-                both = edge_in[step, 0, at, :]
+                both = fringe[at, :]
                 for r in range(rows):
                     moved = pltpu.roll(both, cols - 1 - 2 * r, 1)
                     s = dst[r, at, :] + jnp.where((lane == cols - 1) | (lane == 0), moved, 0.0)
                     dst[r, at, :] = s
                     packed = pack_row(packed, r, s, wlon[r, at, :])
-                edge_out[step + 1, 1, at, :] = packed
+                edge_out[step + 1, 1, at, :] = packed.astype(jnp.bfloat16)
                 return carry
 
+            send_rows(
+                step + 1,
+                dst[0] + jnp.where(at_side, pltpu.roll(both, cols - 1, 1), 0.0),
+                dst[rows - 1]
+                + jnp.where(at_side, pltpu.roll(both, cols - 1 - 2 * (rows - 1), 1), 0.0),
+            )
             lax.fori_loop(0, levels // part, mend, 0)
             edge_copy(step + 1, 0).start()
             edge_copy(step + 1, 1).start()
-            edge_out[step + 1, 2] = split(dst[0], wlat[0])[0]
-            edge_out[step + 1, 3] = split(dst[rows - 1], wlat[rows - 1])[1]
-            edge_copy(step + 1, 2).start()
-            edge_copy(step + 1, 3).start()
         else:
             def finish(t, carry):
                 for j in range(4):
                     r = t * 4 + j
                     for q in range(levels // part):
                         at = pl.ds(q * part, part)
-                        moved = pltpu.roll(edge_in[step, 0, at, :], cols - 1 - 2 * r, 1)
+                        moved = pltpu.roll(fringe[at, :], cols - 1 - 2 * r, 1)
                         dst[r, at, :] = dst[r, at, :] + jnp.where(
                             (lane == cols - 1) | (lane == 0), moved, 0.0
                         )
@@ -358,8 +394,9 @@
             pltpu.VMEM(block, jnp.bfloat16),
             pltpu.VMEM(block, jnp.bfloat16),
             field, field, field, field,
-            pltpu.VMEM((STEPS, 4, levels, cols), jnp.float32),
-            pltpu.VMEM((STEPS, 4, levels, cols), jnp.float32),
+            pltpu.VMEM((STEPS, 4, levels, cols), jnp.bfloat16),
+            pltpu.VMEM((STEPS, 4, levels, cols), jnp.bfloat16),
+            pltpu.VMEM((levels, cols), jnp.float32),
             pltpu.SemaphoreType.DMA((4,)),
             pltpu.SemaphoreType.DMA,
             pltpu.SemaphoreType.DMA((n_dev,)),

time: 56.1 us -> 51.9 us (0.925)
  Pallas kernels: 52.8 us -> 48.6 us
    pallas_call x1, Pallas kernels: 52.8 us -> 48.6 us  [local(): pl.pallas_call(functools.partial(kernel, n_lat, n_lon), out_shape=jax.Sha...]
where the time goes in v2:
time: 51.9 us; the launch traced here: 51.7 us
  Pallas kernels  48.6 us (94%)
  local copies, waits for them, and re-layouts  3.08 us (6%)
    pallas_call x1, Pallas kernels, local(): pl.pallas_call(functools.partial(kernel, n_lat, n_lon), out_shape=jax.Sha...  48.6 us
    unnamed x1, local copies, waits for them, and re-layouts  3.08 us

profile of v2, /device:TPU:0, one launch (start us, length us, event | category | flops | bytes accessed | tf_op | source)
XLA Modules:
  0.0 51.7 jit_solution(6769462578449294772)
XLA Ops:
  0.0 48.6 %assimilate.1 = f32[128,32,128]{2,1,0:T(8,128)} custom-call(s32[4,2048]{1,0:T(4,128)} %bitcast.1, bf16[2048,256]{1,0:T(8,128)(2,1)} %dep_hbm.1, bf16[256,128]{1,0:T(8,128)(2,1)} %cmap.1, f32[128,32,128]{2,1,0:T(8,128)} %adj_hbm.1, f32[128,32,128]{2,1,0:T(8,128)} %wlon_hbm.1, f32[128,32,128]{2,1,0:T(8,128)} %wlat_hbm.1), custom_call_target="tpu_custom_call" | custom-call | tf_op jit(solution)/shard_map/assimilate/pallas_call | solution.py:385
  48.6 3.1 %copy.8 = f32[128,32,128]{2,1,0:T(8,128)} copy(f32[128,32,128]{2,1,0:T(8,128)} %assimilate.1) | data formatting | bytes 4194304
